TPU v7x, 128 devices: a whole 4x4x4 slice. The times are simulated.
128 devices in a mesh: fsdp: 8 (over x_lo, y), tp: 16 (over z, x_hi, core).
Axes of the slice: x: 4 (x_hi: 2, x_lo: 2; x = x_hi * 2 + x_lo), y: 4, z: 4, core: 2. Of those that a mesh axis runs over, the one named last changes fastest.
Arguments:
- prefix_states: bfloat16 [32768, 8192], P('fsdp', 'tp'), may hold values from -40 to 40
- new_states: bfloat16 [128, 8192], P('fsdp', 'tp'), may hold values from -40 to 40
- w_query: bfloat16 [8192, 8192], P('tp', 'fsdp'), may hold values from -0.09375 to 0.09375
- w_keyvalue: bfloat16 [8192, 2048], P('tp', 'fsdp'), may hold values from -0.03125 to 0.03125
- w_output: bfloat16 [8192, 8192], P('tp', 'fsdp'), may hold values from -0.25 to 0.25
- lengths: int32 [8, 4], P('fsdp'), may hold values from 1 to 1024, 3072 in all within a row
Outputs:
- kv_cache: bfloat16 [32768, 2048], P('fsdp', 'tp')
- mixed: bfloat16 [128, 8192], P('fsdp', 'tp')
Inputs may be any that keep to these rules, and one draw needn't show every extreme that they name: `lengths`: in every group some sequence has length 1024.
All inputs are finite; a program needn't handle non-finite values.
Results may differ from a plain program's by a relative error of at most 0.02.
Values may be sent and summed in bfloat16 or wider, within the bound.
No kernel may reach another device: no remote copies, remote signals or barrier semaphores. Data moves between devices by JAX's collectives and lax.ppermute only.
A program may use at most 128 MiB of HBM per device.

v0:
```python
import jax
import jax.numpy as jnp
from jax import lax
from jax.sharding import PartitionSpec as P

HD = 128
NSEQ = 4
L = 1024
STEPS = 4
theta_base = 500000.0
masked_score = -1e30


def partner(block, axis, apart):
    count = lax.axis_size(axis)
    route = []
    for low in range(count):
        high = low | 1 << apart
        if high != low and high < count:
            route += [(low, high), (high, low)]
    return lax.ppermute(block, axis, route)


def rotate(values, positions):
    half_dim = values.shape[-1] // 2
    frequency = theta_base ** (-2.0 * jnp.arange(half_dim, dtype=jnp.float32) / values.shape[-1])
    angles = positions[:, None, None] * frequency[None, None, :]
    cosine = jnp.cos(angles)
    sine_part = jnp.sin(angles)
    lower_half = values[..., :half_dim]
    upper_half = values[..., half_dim:]
    return jnp.concatenate(
        [
            lower_half * cosine - upper_half * sine_part,
            upper_half * cosine + lower_half * sine_part,
        ],
        axis=-1,
    )


def rotate_columns(column_table, positions):
    half_dim = column_table.shape[0] // 2
    frequency = theta_base ** (
        -2.0 * jnp.arange(half_dim, dtype=jnp.float32) / column_table.shape[0]
    )
    angles = frequency[:, None] * positions[None, :]
    cosine = jnp.cos(angles)
    sine_part = jnp.sin(angles)
    lower_half = column_table[:half_dim]
    upper_half = column_table[half_dim:]
    return jnp.concatenate(
        [
            lower_half * cosine - upper_half * sine_part,
            upper_half * cosine + lower_half * sine_part,
        ],
        axis=0,
    )


def body(prefix_states, new_states, w_query, w_keyvalue, w_output, lengths):
    tp_count = lax.axis_size("tp")
    my_index = lax.axis_index("tp")
    token_count = prefix_states.shape[0]
    fresh_count = new_states.shape[0]
    seq_lengths = lengths[0]
    score_scale = HD ** (-0.5)
    kv_weight = lax.all_gather(w_keyvalue, "fsdp", axis=1, tiled=True)
    kv_width = kv_weight.shape[1]
    query_term = jnp.dot(
        new_states,
        lax.all_gather(w_query, "fsdp", axis=1, tiled=True),
        preferred_element_type=jnp.float32,
    )
    fresh_term = jnp.dot(new_states, kv_weight, preferred_element_type=jnp.float32)
    fresh_positions = (
        jnp.repeat(seq_lengths, STEPS) + jnp.tile(jnp.arange(STEPS, dtype=jnp.int32), NSEQ)
    ).astype(jnp.float32)
    own_rows = kv_width // tp_count
    block_count = own_rows // HD
    block_kind = (my_index * block_count + jnp.arange(block_count, dtype=jnp.int32)) % 2
    cache_sum = lax.psum_scatter(
        lax.dot_general(
            kv_weight, prefix_states, (((0,), (1,)), ((), ())), preferred_element_type=jnp.float32
        ).astype(jnp.bfloat16),
        "tp",
        scatter_dimension=0,
        tiled=True,
    ).astype(jnp.float32)
    slot_positions = (jnp.arange(token_count, dtype=jnp.int32) % L).astype(jnp.float32)
    cache_blocks = cache_sum.reshape(block_count, HD, token_count)
    rotated_blocks = jax.vmap(lambda block_data: rotate_columns(block_data, slot_positions))(
        cache_blocks
    )
    cache_mine = jnp.where((block_kind == 0)[:, None, None], rotated_blocks, cache_blocks).astype(
        jnp.bfloat16
    )
    query_sum, fresh_sum = (
        lax.psum_scatter(query_term, "tp", scatter_dimension=1, tiled=True),
        lax.psum_scatter(fresh_term, "tp", scatter_dimension=1, tiled=True),
    )
    fresh_blocks = fresh_sum.reshape(fresh_count, block_count, HD)
    fresh_rotated = rotate(fresh_blocks, fresh_positions)
    fresh_mine = jnp.where((block_kind == 0)[None, :, None], fresh_rotated, fresh_blocks).astype(
        jnp.bfloat16
    )
    cache_other, fresh_other = partner((cache_mine, fresh_mine), "tp", 0)
    holds_keys = my_index % 2 == 0
    key_table = jnp.where(holds_keys, cache_mine[0], cache_other[0])
    value_table = jnp.where(holds_keys, cache_other[0], cache_mine[0])
    fresh_keys = jnp.where(holds_keys, fresh_mine[:, 0], fresh_other[:, 0])
    fresh_values = jnp.where(holds_keys, fresh_other[:, 0], fresh_mine[:, 0])
    cache_out = cache_mine.reshape(own_rows, token_count).T
    local_heads = query_sum.shape[1] // HD
    query_rot = rotate(query_sum.reshape(fresh_count, local_heads, HD), fresh_positions).astype(
        jnp.bfloat16
    )
    query_four = query_rot.reshape(NSEQ, STEPS, local_heads, HD)
    prefix_scores = (
        jnp.einsum(
            "sjhd,dsl->sjhl",
            query_four,
            key_table.reshape(HD, NSEQ, L),
            preferred_element_type=jnp.float32,
        )
        * score_scale
    )
    live_keys = jnp.arange(L, dtype=jnp.int32)[None, :] < seq_lengths[:, None]
    prefix_scores = jnp.where(live_keys[:, None, None, :], prefix_scores, masked_score)
    fresh_scores = (
        jnp.einsum(
            "sjhd,sid->sjhi",
            query_four,
            fresh_keys.reshape(NSEQ, STEPS, HD),
            preferred_element_type=jnp.float32,
        )
        * score_scale
    )
    causal = jnp.arange(STEPS)[None, :] <= jnp.arange(STEPS)[:, None]
    fresh_scores = jnp.where(causal[None, :, None, :], fresh_scores, masked_score)
    row_max = jnp.maximum(jnp.max(prefix_scores, axis=-1), jnp.max(fresh_scores, axis=-1))
    prefix_weight = jnp.exp(prefix_scores - row_max[..., None])
    fresh_weight = jnp.exp(fresh_scores - row_max[..., None])
    denominator = jnp.sum(prefix_weight, axis=-1) + jnp.sum(fresh_weight, axis=-1)
    numerator = jnp.einsum(
        "sjhl,dsl->sjhd",
        prefix_weight.astype(jnp.bfloat16),
        value_table.reshape(HD, NSEQ, L),
        preferred_element_type=jnp.float32,
    )
    numerator = numerator + jnp.einsum(
        "sjhi,sid->sjhd",
        fresh_weight.astype(jnp.bfloat16),
        fresh_values.reshape(NSEQ, STEPS, HD),
        preferred_element_type=jnp.float32,
    )
    attended = (
        (numerator / denominator[..., None])
        .reshape(fresh_count, local_heads * HD)
        .astype(jnp.bfloat16)
    )
    output_term = jnp.dot(
        attended,
        lax.all_gather(w_output, "fsdp", axis=1, tiled=True),
        preferred_element_type=jnp.float32,
    )
    output_total = lax.psum(output_term, "tp")
    feature_width = output_total.shape[1] // tp_count
    mixed = lax.dynamic_slice_in_dim(output_total, my_index * feature_width, feature_width, 1)
    return (cache_out, mixed.astype(jnp.bfloat16))


def solution(mesh):
    in_specs = (
        P("fsdp", "tp"),
        P("fsdp", "tp"),
        P("tp", "fsdp"),
        P("tp", "fsdp"),
        P("tp", "fsdp"),
        P("fsdp", None),
    )
    out_specs = (P("fsdp", "tp"), P("fsdp", "tp"))
    return jax.shard_map(body, mesh=mesh, in_specs=in_specs, out_specs=out_specs, check_vma=False)
```

profile of v0, /device:TPU:0, one launch (start us, length us, event | category | flops | bytes accessed | tf_op | source)
XLA Modules:
  0.0 613.5 jit_solution(11667397842133907889)
XLA Ops:
  7.2 0.7 all-gather.4.cloned.1.call-update
  8.0 0.7 all-gather.6.cloned.1.call-update
  8.7 48.1 %all-gather.4.cloned.1.call-done = bf16[512,2048]{1,0:T(8,128)(2,1)} async-done(((bf16[512,256]{1,0:T(8,128)(2,1)}), bf16[512,2048]{1,0:T(8,128)(2,1)}) %all-gather.4.cloned.1.call-update) | async-done | bytes 2097168 | tf_op jit(solution)/shard_map/all_gather | solution.py:67
  56.8 14.9 %convolution_convert_fusion = bf16[2048,4096]{1,0:T(8,128)(2,1)} fusion(bf16[512,2048]{1,0:T(8,128)(2,1)} %all-gather.4.cloned.1.call-done, bf16[4096,512]{1,0:T(8,128)(2,1)} %param.6), kind=kOutput, calls=%fused_computation | convolution fusion | flops 8598323200 | bytes 23068672 | tf_op jit(solution)/shard_map/dot_general | solution.py:82
  71.8 1.5 copy-done.2
  73.3 1.0 fusion.57
  74.5 77.4 %all-gather.6.cloned.1.call-done = bf16[512,8192]{1,0:T(8,128)(2,1)} async-done(((bf16[512,1024]{1,0:T(8,128)(2,1)}), bf16[512,8192]{1,0:T(8,128)(2,1)}) %all-gather.6.cloned.1.call-update) | async-done | bytes 8388624 | tf_op jit(solution)/shard_map/all_gather | solution.py:71
  151.8 5.4 fusion.56
  157.3 0.5 all-gather.8.cloned.1.call-update
  158.0 0.1 multiply_cosine_fusion.2
  158.2 144.2 %reduce-scatter.4.cloned.1.call-done = bf16[128,4096]{1,0:T(8,128)(2,1)} async-done(((bf16[2048,4096]{1,0:T(8,128)(2,1)}), bf16[128,4096]{1,0:T(8,128)(2,1)}) %reduce-scatter.4.cloned.1.call-update) | async-done | bytes 1048592 | tf_op jit(solution)/shard_map/reduce_scatter | solution.py:81
  302.3 1.5 convert_bitcast_fusion
  303.8 4.2 fusion.10
  308.1 0.3 fusion
  308.6 56.8 %reduce-scatter.8.cloned.1.call-done = f32[16,128]{1,0:T(8,128)} async-done(((f32[16,2048]{1,0:T(8,128)}), f32[16,128]{1,0:T(8,128)}) %reduce-scatter.8.cloned.1.call-update) | async-done | bytes 8208 | tf_op jit(solution)/shard_map/reduce_scatter | solution.py:99
  365.4 0.9 fusion.44
  366.3 0.1 fusion.47
  366.3 0.2 collective-permute-start.1
  366.6 67.9 %reduce-scatter.6.cloned.1.call-done = f32[16,512]{1,0:T(8,128)} async-done(((f32[16,8192]{1,0:T(8,128)}), f32[16,512]{1,0:T(8,128)}) %reduce-scatter.6.cloned.1.call-update) | async-done | bytes 32784 | tf_op jit(solution)/shard_map/reduce_scatter | solution.py:98
  434.5 0.8 reshape.323
  435.2 0.1 subtract_convert_fusion
  435.3 0.3 fusion.55
  435.7 1.3 copy.13
  437.0 0.8 squeeze.6
  437.8 0.9 fusion.54
  438.7 0.2 fusion.23
  438.9 0.2 fusion.30
  439.1 0.8 fusion.8
  440.0 86.9 %all-gather.8.cloned.1.call-done = bf16[512,8192]{1,0:T(8,128)(2,1)} async-done(((bf16[512,1024]{1,0:T(8,128)(2,1)}), bf16[512,8192]{1,0:T(8,128)(2,1)}) %all-gather.8.cloned.1.call-update) | async-done | bytes 8388624 | tf_op jit(solution)/shard_map/all_gather | solution.py:163
  526.9 4.6 fusion.32
  531.5 74.5 %all-reduce.1 = bf16[16,8192]{1,0:T(8,128)(2,1)S(1)} all-reduce(f32[16,8192]{1,0:T(8,128)S(1)} %fusion.32), channel_id=1, replica_groups=mesh['fsdp'=8,'tp'=16] {'tp'}, use_global_device_ids=true, to_apply=%region_7.8 | all-reduce | flops 131072 | bytes 786432 | tf_op jit(solution)/shard_map/psum | solution.py:166
  606.0 0.6 dynamic-slice_convert_fusion
  (28 shorter events, 0.7 us)
Async XLA Ops:
  7.2 64.7 %copy-start = (bf16[16,512]{1,0:T(8,128)(2,1)S(1)}, bf16[16,512]{1,0:T(8,128)(2,1)}, u32[]{:S(2)}) copy-start(bf16[16,512]{1,0:T(8,128)(2,1)} %param.7) | copy-start | bytes 49156
  7.2 49.7 %all-gather.4.cloned.1.call-start = ((), (), s32[]{:S(2)}) async-start(), calls=%async_computation.3 | async-start | bytes 2359296 | tf_op jit(solution)/shard_map/all_gather | solution.py:67
  7.9 143.9 %all-gather.6.cloned.1.call-start = ((), (), s32[]{:S(2)}) async-start(), calls=%async_computation.5 | async-start | bytes 9437184 | tf_op jit(solution)/shard_map/all_gather | solution.py:71
  8.7 293.6 %reduce-scatter.4.cloned.1.call-start = ((), (), s32[]{:S(2)}) async-start(), calls=%async_computation.4 | async-start | bytes 17825792 | tf_op jit(solution)/shard_map/reduce_scatter | solution.py:81
  71.8 1.6 copy-start.2
  71.8 293.6 %reduce-scatter.8.cloned.1.call-start = ((), (), s32[]{:S(2)}) async-start(), calls=%async_computation.7 | async-start | bytes 139264 | tf_op jit(solution)/shard_map/reduce_scatter | solution.py:99
  74.4 83.4 %copy-start.3 = (s32[1,4]{1,0:T(1,128)S(1)}, s32[1,4]{1,0:T(1,128)}, u32[]{:S(2)}) copy-start(s32[1,4]{1,0:T(1,128)} %param.11) | copy-start | bytes 52
  74.4 360.0 %reduce-scatter.6.cloned.1.call-start = ((), (), s32[]{:S(2)}) async-start(), calls=%async_computation.6 | async-start | bytes 557056 | tf_op jit(solution)/shard_map/reduce_scatter | solution.py:98
  157.2 369.7 %all-gather.8.cloned.1.call-start = ((), (), s32[]{:S(2)}) async-start(), calls=%async_computation.8 | async-start | bytes 9437184 | tf_op jit(solution)/shard_map/all_gather | solution.py:163
  302.3 5.8 copy-start.1
  308.4 128.6 %collective-permute-start = (bf16[1,128,4096]{2,1,0:T(8,128)(2,1)S(1)}, bf16[1,128,4096]{2,1,0:T(8,128)(2,1)S(1)}, u32[]{:S(2)}, u32[]{:S(2)}) collective-permute-start(bf16[1,128,4096]{2,1,0:T(8,128)(2,1)S(1)} %bitcast.69), channel_id=1, source_target_pairs={{0,1},{1,0},{2,3},{3,2},{4,5},{5,4},{6,7},{7,6},{8,9},{9,8},{10,11... | collective-permute-start | bytes 3145736 | tf_op jit(solution)/shard_map/ppermute | solution.py:21
  366.3 69.0 %collective-permute-start.1 = (bf16[16,1,128]{2,0,1:T(8,128)(2,1)S(1)}, bf16[16,1,128]{2,0,1:T(8,128)(2,1)S(1)}, u32[]{:S(2)}, u32[]{:S(2)}) collective-permute-start(bf16[16,1,128]{2,0,1:T(8,128)(2,1)S(1)} %bitcast.79), channel_id=1, source_target_pairs={{0,1},{1,0},{2,3},{3,2},{4,5},{5,4},{6,7},{7,6},{8,9},{9,8},{10,11... | collective-permute-start | bytes 12296 | tf_op jit(solution)/shard_map/ppermute | solution.py:21
Sparse Core Ops, SparseCore 0:
  9.6 47.2 all-gather.3
  58.5 93.3 all-gather.5
  156.2 146.1 reduce-scatter.3
  305.7 59.5 reduce-scatter.7
  369.5 64.9 reduce-scatter.5
  436.0 90.8 all-gather.7
where the time goes:
time: 614 us; the launch traced here: 613 us
  waiting for transfers between devices  483 us (79%)
  blocking collectives  74.5 us (12%)
  matrix products  28.1 us (5%)
  between operations  14.3 us (2%)
  other arithmetic  7.71 us (1%)
    reduce_scatter x1, waiting for transfers between devices, body(): lax.psum_scatter(lax.dot_general(kv_weight, prefix_states, (((0,), (1,)),...  144 us
    all_gather x1, waiting for transfers between devices, body(): lax.all_gather(w_output, 'fsdp', axis=1, tiled=True)  86.9 us
    all_gather x1, waiting for transfers between devices, body(): lax.all_gather(w_query, 'fsdp', axis=1, tiled=True)  77.4 us
    psum x1, blocking collectives, body(): output_total = lax.psum(output_term, 'tp')  74.5 us
    reduce_scatter x1, waiting for transfers between devices, body(): lax.psum_scatter(query_term, 'tp', scatter_dimension=1, tiled=True)  67.9 us
    reduce_scatter x1, waiting for transfers between devices, body(): lax.psum_scatter(fresh_term, 'tp', scatter_dimension=1, tiled=True)  56.8 us
    all_gather x1, waiting for transfers between devices, body(): kv_weight = lax.all_gather(w_keyvalue, 'fsdp', axis=1, tiled=True)  48.1 us
    dot_general x1, matrix products, body(): lax.dot_general(kv_weight, prefix_states, (((0,), (1,)), ((), ())), prefe...  14.9 us
  transfers between devices with their start and end apart: 8, of which 6 were waited for; matrix products, arithmetic and copies ran while one was open for 6% of the time, Pallas kernels for 0%

commit v1 on v0

--- a/solution.py
+++ b/solution.py
@@ -163,7 +163,7 @@
         lax.all_gather(w_output, "fsdp", axis=1, tiled=True),
         preferred_element_type=jnp.float32,
     )
-    output_total = lax.psum(output_term, "tp")
+    output_total = lax.all_gather(output_term, "tp").sum(axis=0)
     feature_width = output_total.shape[1] // tp_count
     mixed = lax.dynamic_slice_in_dim(output_total, my_index * feature_width, feature_width, 1)
     return (cache_out, mixed.astype(jnp.bfloat16))

time: 614 us -> 617 us (level)
  blocking collectives: 74.5 us -> 0 us
  waiting for transfers between devices: 483 us -> 555 us
    psum x1 -> x0, blocking collectives: 74.5 us -> none  [body(): output_total = lax.psum(output_term, 'tp')]
    all_gather x0 -> x1, waiting for transfers between devices: none -> 70.4 us  [body(): output_total = lax.all_gather(output_term, 'tp').sum(axis=0)]
  transfers between devices with their start and end apart: 8 -> 9, of which waited for: 6 -> 7; matrix products, arithmetic and copies ran while one was open for 6% -> 6% of each run, Pallas kernels for 0% -> 0%
where the time goes in v1:
time: 617 us; the launch traced here: 615 us
  waiting for transfers between devices  555 us (90%)
  matrix products  29 us (5%)
  between operations  14.3 us (2%)
  other arithmetic  11.5 us (2%)
    reduce_scatter x1, waiting for transfers between devices, body(): lax.psum_scatter(lax.dot_general(kv_weight, prefix_states, (((0,), (1,)),...  144 us
    all_gather x1, waiting for transfers between devices, body(): lax.all_gather(w_output, 'fsdp', axis=1, tiled=True)  88.2 us
    all_gather x1, waiting for transfers between devices, body(): lax.all_gather(w_query, 'fsdp', axis=1, tiled=True)  77.4 us
    all_gather x1, waiting for transfers between devices, body(): output_total = lax.all_gather(output_term, 'tp').sum(axis=0)  70.4 us
    reduce_scatter x1, waiting for transfers between devices, body(): lax.psum_scatter(query_term, 'tp', scatter_dimension=1, tiled=True)  67.9 us
    reduce_scatter x1, waiting for transfers between devices, body(): lax.psum_scatter(fresh_term, 'tp', scatter_dimension=1, tiled=True)  56.8 us
    all_gather x1, waiting for transfers between devices, body(): kv_weight = lax.all_gather(w_keyvalue, 'fsdp', axis=1, tiled=True)  48.1 us
    dot_general x1, matrix products, body(): lax.dot_general(kv_weight, prefix_states, (((0,), (1,)), ((), ())), prefe...  14.9 us
  transfers between devices with their start and end apart: 9, of which 7 were waited for; matrix products, arithmetic and copies ran while one was open for 6% of the time, Pallas kernels for 0%

profile of v1, /device:TPU:0, one launch (start us, length us, event | category | flops | bytes accessed | tf_op | source)
XLA Modules:
  0.0 615.5 jit_solution(33329522564441813)
XLA Ops:
  7.2 0.7 all-gather.6.cloned.1.call-update
  8.0 0.7 all-gather.8.cloned.1.call-update
  8.7 48.1 %all-gather.6.cloned.1.call-done = bf16[512,2048]{1,0:T(8,128)(2,1)} async-done(((bf16[512,256]{1,0:T(8,128)(2,1)}), bf16[512,2048]{1,0:T(8,128)(2,1)}) %all-gather.6.cloned.1.call-update) | async-done | bytes 2097168 | tf_op jit(solution)/shard_map/all_gather | solution.py:67
  56.8 14.9 %convolution_convert_fusion = bf16[2048,4096]{1,0:T(8,128)(2,1)} fusion(bf16[512,2048]{1,0:T(8,128)(2,1)} %all-gather.6.cloned.1.call-done, bf16[4096,512]{1,0:T(8,128)(2,1)} %param.6), kind=kOutput, calls=%fused_computation | convolution fusion | flops 8598323200 | bytes 23068672 | tf_op jit(solution)/shard_map/dot_general | solution.py:82
  71.8 1.5 copy-done.2
  73.3 1.0 fusion.57
  74.5 77.4 %all-gather.8.cloned.1.call-done = bf16[512,8192]{1,0:T(8,128)(2,1)} async-done(((bf16[512,1024]{1,0:T(8,128)(2,1)}), bf16[512,8192]{1,0:T(8,128)(2,1)}) %all-gather.8.cloned.1.call-update) | async-done | bytes 8388624 | tf_op jit(solution)/shard_map/all_gather | solution.py:71
  151.8 5.4 fusion.56
  157.3 0.5 all-gather.10.cloned.1.call-update
  158.1 0.1 multiply_cosine_fusion.2
  158.2 144.2 %reduce-scatter.4.cloned.1.call-done = bf16[128,4096]{1,0:T(8,128)(2,1)} async-done(((bf16[2048,4096]{1,0:T(8,128)(2,1)}), bf16[128,4096]{1,0:T(8,128)(2,1)}) %reduce-scatter.4.cloned.1.call-update) | async-done | bytes 1048592 | tf_op jit(solution)/shard_map/reduce_scatter | solution.py:81
  302.4 1.5 convert_bitcast_fusion
  303.9 4.2 fusion.10
  308.2 0.3 fusion
  308.7 56.8 %reduce-scatter.8.cloned.1.call-done = f32[16,128]{1,0:T(8,128)} async-done(((f32[16,2048]{1,0:T(8,128)}), f32[16,128]{1,0:T(8,128)}) %reduce-scatter.8.cloned.1.call-update) | async-done | bytes 8208 | tf_op jit(solution)/shard_map/reduce_scatter | solution.py:99
  365.5 0.9 fusion.44
  366.4 0.1 fusion.47
  366.5 0.2 collective-permute-start.1
  366.7 67.9 %reduce-scatter.6.cloned.1.call-done = f32[16,512]{1,0:T(8,128)} async-done(((f32[16,8192]{1,0:T(8,128)}), f32[16,512]{1,0:T(8,128)}) %reduce-scatter.6.cloned.1.call-update) | async-done | bytes 32784 | tf_op jit(solution)/shard_map/reduce_scatter | solution.py:98
  434.6 0.8 reshape.323
  435.4 0.3 fusion.55
  435.8 0.8 squeeze.6
  436.6 0.9 fusion.54
  437.5 0.2 fusion.23
  437.8 0.2 fusion.30
  438.0 0.8 fusion.8
  438.8 88.2 %all-gather.10.cloned.1.call-done = bf16[512,8192]{1,0:T(8,128)(2,1)} async-done(((bf16[512,1024]{1,0:T(8,128)(2,1)}), bf16[512,8192]{1,0:T(8,128)(2,1)}) %all-gather.10.cloned.1.call-update) | async-done | bytes 8388624 | tf_op jit(solution)/shard_map/all_gather | solution.py:163
  527.0 5.4 fusion.32
  532.5 1.3 copy.13
  533.8 70.4 %all-gather.12.cloned.1.call-done = f32[256,8192]{1,0:T(8,128)} async-done(((f32[16,8192]{1,0:T(8,128)}), f32[256,8192]{1,0:T(8,128)}) %all-gather.12.cloned.1.call-update) | async-done | bytes 8388624 | tf_op jit(solution)/shard_map/all_gather | solution.py:166
  604.2 3.8 reduce_sum.29
  608.0 0.6 dynamic-slice_convert_fusion
  (31 shorter events, 0.9 us)
Async XLA Ops:
  7.2 64.7 %copy-start = (bf16[16,512]{1,0:T(8,128)(2,1)S(1)}, bf16[16,512]{1,0:T(8,128)(2,1)}, u32[]{:S(2)}) copy-start(bf16[16,512]{1,0:T(8,128)(2,1)} %param.7) | copy-start | bytes 49156
  7.2 49.7 %all-gather.6.cloned.1.call-start = ((), (), s32[]{:S(2)}) async-start(), calls=%async_computation.3 | async-start | bytes 2359296 | tf_op jit(solution)/shard_map/all_gather | solution.py:67
  7.9 143.9 %all-gather.8.cloned.1.call-start = ((), (), s32[]{:S(2)}) async-start(), calls=%async_computation.5 | async-start | bytes 9437184 | tf_op jit(solution)/shard_map/all_gather | solution.py:71
  8.7 293.7 %reduce-scatter.4.cloned.1.call-start = ((), (), s32[]{:S(2)}) async-start(), calls=%async_computation.4 | async-start | bytes 17825792 | tf_op jit(solution)/shard_map/reduce_scatter | solution.py:81
  71.8 1.6 copy-start.2
  71.8 293.7 %reduce-scatter.8.cloned.1.call-start = ((), (), s32[]{:S(2)}) async-start(), calls=%async_computation.7 | async-start | bytes 139264 | tf_op jit(solution)/shard_map/reduce_scatter | solution.py:99
  74.4 83.5 %copy-start.3 = (s32[1,4]{1,0:T(1,128)S(1)}, s32[1,4]{1,0:T(1,128)}, u32[]{:S(2)}) copy-start(s32[1,4]{1,0:T(1,128)} %param.11) | copy-start | bytes 52
  74.4 360.1 %reduce-scatter.6.cloned.1.call-start = ((), (), s32[]{:S(2)}) async-start(), calls=%async_computation.6 | async-start | bytes 557056 | tf_op jit(solution)/shard_map/reduce_scatter | solution.py:98
  157.2 369.8 %all-gather.10.cloned.1.call-start = ((), (), s32[]{:S(2)}) async-start(), calls=%async_computation.8 | async-start | bytes 9437184 | tf_op jit(solution)/shard_map/all_gather | solution.py:163
  157.8 446.4 %all-gather.12.cloned.1.call-start = ((), (), s32[]{:S(2)}) async-start(), calls=%async_computation.9 | async-start | bytes 8912896 | tf_op jit(solution)/shard_map/all_gather | solution.py:166
  302.4 5.8 copy-start.1
  308.5 127.3 %collective-permute-start = (bf16[1,128,4096]{2,1,0:T(8,128)(2,1)S(1)}, bf16[1,128,4096]{2,1,0:T(8,128)(2,1)S(1)}, u32[]{:S(2)}, u32[]{:S(2)}) collective-permute-start(bf16[1,128,4096]{2,1,0:T(8,128)(2,1)S(1)} %bitcast.71), channel_id=1, source_target_pairs={{0,1},{1,0},{2,3},{3,2},{4,5},{5,4},{6,7},{7,6},{8,9},{9,8},{10,11... | collective-permute-start | bytes 3145736 | tf_op jit(solution)/shard_map/ppermute | solution.py:21
  366.5 69.0 %collective-permute-start.1 = (bf16[16,1,128]{2,0,1:T(8,128)(2,1)S(1)}, bf16[16,1,128]{2,0,1:T(8,128)(2,1)S(1)}, u32[]{:S(2)}, u32[]{:S(2)}) collective-permute-start(bf16[16,1,128]{2,0,1:T(8,128)(2,1)S(1)} %bitcast.81), channel_id=1, source_target_pairs={{0,1},{1,0},{2,3},{3,2},{4,5},{5,4},{6,7},{7,6},{8,9},{9,8},{10,11... | collective-permute-start | bytes 12296 | tf_op jit(solution)/shard_map/ppermute | solution.py:21
Sparse Core Ops, SparseCore 0:
  9.6 47.2 all-gather.5
  58.5 93.3 all-gather.7
  156.2 146.1 reduce-scatter.3
  305.8 59.6 reduce-scatter.7
  369.6 64.9 reduce-scatter.5
  436.1 90.8 all-gather.9
  532.6 71.5 all-gather.11
